TPU v7x, 256 devices: a whole 4x4x8 slice. The times are simulated.
256 devices in a mesh: dom: 8 (over y, core), feat: 32 (over z, x).
Axes of the slice: x: 4, y: 4, z: 8, core: 2. Of those that a mesh axis runs over, the one named last changes fastest.
Arguments:
- node_feats: bfloat16 [1024, 32768], P('feat', 'dom'), may hold values from -6 to 6
- send_rows: int32 [8192], P('dom'), may hold values from 0 to 4095
- hub_rows: int32 [1024], P('dom'), may hold values from 0 to 4095
- tile_dst: int32 [4096], P('dom'), may hold values from 0 to 7
- tile_src: int32 [4096], P('dom'), may hold values from 0 to 47
- tile_count: int32 [8], P('dom'), may hold values from 128 to 512, as said below
- tile_vals: bfloat16 [4096, 128, 128], P('dom'), may hold values from -0.0625 to 0.0625
- w_self: bfloat16 [1024, 1024], P('feat'), may hold values from -0.1875 to 0.1875
- w_neigh: bfloat16 [1024, 1024], P('feat'), may hold values from -0.1875 to 0.1875
- bias_vec: float32 [1024], P('feat'), may hold values from -3 to 3
- cotangent: bfloat16 [1024, 8192], P('feat', 'dom'), may hold values from -6 to 6
Outputs:
- activations: bfloat16 [1024, 8192], P('feat', 'dom')
- grad_feats: float32 [1024, 32768], P('feat', 'dom')
- grad_w_self: float32 [1024, 1024], P('feat')
- grad_w_neigh: float32 [1024, 1024], P('feat')
- grad_bias: float32 [1024], P('feat')
Inputs may be any that keep to these rules, and one draw needn't show every extreme that they name: `tile_count`: every partition has at least 128 live slots, and some partition has all 512 live; slots at or past the count are not edges: their tile_vals may hold any values and must be ignored.
All inputs are finite; a program needn't handle non-finite values.
Results may differ from a plain program's by a relative error of at most 0.0075.
Values may be sent and summed in bfloat16 or wider, within the bound.
A program may use at most 128 MiB of HBM per device.

v0:
```python
import jax
import jax.numpy as jnp
from jax import lax
from jax.sharding import PartitionSpec as P


def contract_first(left, right):
    return lax.dot_general(
        left, right, (((0,), (0,)), ((), ())), preferred_element_type=jnp.float32
    )


def contract_last(left, right):
    return lax.dot_general(
        left, right, (((1,), (1,)), ((), ())), preferred_element_type=jnp.float32
    )


def body(
    node_feats,
    send_rows,
    hub_rows,
    tile_dst,
    tile_src,
    tile_count,
    tile_vals,
    w_self,
    w_neigh,
    bias_vec,
    cotangent,
):
    feat_cols = node_feats.shape[0]
    own_rows = node_feats.shape[1]
    dst_rows = cotangent.shape[1]
    sent_total = send_rows.shape[0]
    outgoing = jnp.take(node_feats, send_rows, axis=1)
    halo_cols = lax.all_to_all(outgoing, "dom", split_axis=1, concat_axis=1, tiled=True)
    hub_cols = lax.all_gather(jnp.take(node_feats, hub_rows, axis=1), "dom", axis=1, tiled=True)
    source_table = jnp.concatenate([node_feats, halo_cols, hub_cols], axis=1)
    tile_total = source_table.shape[1] // 128
    dst_tiles = dst_rows // 128
    live_mask = (jnp.arange(tile_dst.shape[0]) < tile_count[0]).astype(jnp.float32)
    dst_hot = (tile_dst[:, None] == jnp.arange(dst_tiles)[None, :]).astype(jnp.float32) * live_mask[
        :, None
    ]
    src_hot = (tile_src[:, None] == jnp.arange(tile_total)[None, :]).astype(
        jnp.float32
    ) * live_mask[:, None]
    picked = source_table.reshape(feat_cols, tile_total, 128)[:, tile_src, :]
    products = jnp.einsum("fkj,kij->fki", picked, tile_vals, preferred_element_type=jnp.float32)
    summed = jnp.einsum("fki,ku->fui", products, dst_hot, precision=lax.Precision.HIGHEST)
    aggregate = summed.reshape(feat_cols, dst_rows).astype(jnp.bfloat16)
    dst_feats = node_feats[:, :dst_rows]
    whole_self, whole_agg = (
        lax.all_gather(dst_feats, "feat", axis=0, tiled=True),
        lax.all_gather(aggregate, "feat", axis=0, tiled=True),
    )
    pre_act = (
        jnp.dot(w_self, whole_self, preferred_element_type=jnp.float32)
        + jnp.dot(w_neigh, whole_agg, preferred_element_type=jnp.float32)
        + bias_vec[:, None]
    )
    sig_val = jax.nn.sigmoid(pre_act)
    activations = (pre_act * sig_val).astype(jnp.bfloat16)
    grad_pre = (cotangent.astype(jnp.float32) * sig_val * (1.0 + pre_act * (1.0 - sig_val))).astype(
        jnp.bfloat16
    )
    local_self = contract_last(grad_pre, whole_self)
    local_neigh = contract_last(grad_pre, whole_agg)
    local_bias = jnp.sum(grad_pre.astype(jnp.float32), axis=1)
    grad_w_self, grad_w_neigh, grad_bias = lax.psum((local_self, local_neigh, local_bias), "dom")
    both_grads = lax.psum_scatter(
        jnp.concatenate(
            [contract_first(w_self, grad_pre), contract_first(w_neigh, grad_pre)], axis=1
        ),
        "feat",
        scatter_dimension=0,
        tiled=True,
    )
    grad_self_in = both_grads[:, :dst_rows]
    grad_agg = both_grads[:, dst_rows:].astype(jnp.bfloat16)
    upstream = grad_agg.reshape(feat_cols, dst_tiles, 128)[:, tile_dst, :]
    back_terms = jnp.einsum("fki,kij->fkj", upstream, tile_vals, preferred_element_type=jnp.float32)
    placed = jnp.einsum("fkj,kt->ftj", back_terms, src_hot, precision=lax.Precision.HIGHEST)
    grad_table = placed.reshape(feat_cols, tile_total * 128)
    halo_grad = grad_table[:, own_rows : own_rows + sent_total]
    hub_grad = grad_table[:, own_rows + sent_total :]
    returned = lax.all_to_all(
        halo_grad.astype(jnp.bfloat16), "dom", split_axis=1, concat_axis=1, tiled=True
    ).astype(halo_grad.dtype)
    hub_total = lax.psum_scatter(
        hub_grad.astype(jnp.bfloat16), "dom", scatter_dimension=1, tiled=True
    ).astype(jnp.float32)
    grad_feats = grad_table[:, :own_rows]
    grad_feats = grad_feats.at[:, send_rows].add(returned)
    grad_feats = grad_feats.at[:, hub_rows].add(hub_total)
    grad_feats = grad_feats.at[:, :dst_rows].add(grad_self_in)
    return (activations, grad_feats, grad_w_self, grad_w_neigh, grad_bias)


def solution(mesh):
    return jax.shard_map(
        body,
        mesh=mesh,
        in_specs=(
            P("feat", "dom"),
            P("dom"),
            P("dom"),
            P("dom"),
            P("dom"),
            P("dom"),
            P("dom", None, None),
            P("feat", None),
            P("feat", None),
            P("feat"),
            P("feat", "dom"),
        ),
        out_specs=(P("feat", "dom"), P("feat", "dom"), P("feat", None), P("feat", None), P("feat")),
        check_vma=False,
    )
```

profile of v0, /device:TPU:2, one launch (start us, length us, event | category | flops | bytes accessed | tf_op | source)
XLA Modules:
  0.0 555.3 jit_solution(6041104265866286545)
XLA Ops:
  7.2 1.5 slice.40
  8.7 1.4 copy.77
  10.9 3.2 gather_fusion
  15.5 4.5 all-to-all-start
  22.8 13.7 %all_gather.10 = bf16[32,1024]{0,1:T(8,128)(2,1)S(1)} all-gather(bf16[32,128]{0,1:T(8,128)(2,1)S(1)} %select_bitcast_fusion), channel_id=1, replica_groups=mesh['dom'=8,'feat'=32] {'dom'}, dimensions={1}, use_global_device_ids=true | all-gather | bytes 73728 | tf_op jit(solution)/shard_map/all_gather | solution.py:38
  37.3 1.0 copy_bitcast_fusion.1
  38.4 3.5 gather_fusion.2
  41.8 13.0 %fusion.8 = f32[32,512,128]{2,0,1:T(8,128)S(1)} fusion(bf16[512,128,128]{2,1,0:T(8,128)(2,1)} %param.19, bf16[512,32,128]{2,1,0:T(8,128)(2,1)} %gather_fusion.2), kind=kOutput, calls=%fused_computation.15 | convolution fusion | flops 536870912 | bytes 29360128 | tf_op jit(solution)/shard_map/fkj,kij->fki/dot_general | solution.py:50
  54.8 8.6 %fusion.16 = bf16[8,32,128]{2,0,1:T(8,128)(2,1)S(1)} fusion(f32[32,512,128]{2,0,1:T(8,128)S(1)} %fusion.8, f32[512]{0:T(512)S(1)} %fusion.30, s32[512]{0:T(512)S(1)} %copy-done.6), kind=kOutput, calls=%fused_computation.22 | convolution fusion | flops 201367552 | bytes 8458240 | tf_op jit(solution)/shard_map/fki,ku->fui/dot_general | solution.py:51
  64.3 26.6 %all-gather.3.cloned.1.call-done = bf16[1024,1024]{1,0:T(8,128)(2,1)} async-done(((bf16[32,1024]{1,0:T(8,128)(2,1)}), bf16[1024,1024]{1,0:T(8,128)(2,1)}) %all-gather.3.cloned.1.call-update) | async-done | bytes 2097168 | tf_op jit(solution)/shard_map/all_gather | solution.py:55
  90.9 2.1 fusion.35
  93.0 76.2 %all-gather.5.cloned.1.call-done = bf16[1024,1024]{1,0:T(8,128)(2,1)} async-done(((bf16[32,1024]{1,0:T(8,128)(2,1)}), bf16[1024,1024]{1,0:T(8,128)(2,1)}) %all-gather.5.cloned.1.call-update) | async-done | bytes 2097168 | tf_op jit(solution)/shard_map/all_gather | solution.py:56
  169.2 2.8 convert_reduce_fusion
  173.5 4.1 pad_maximum_fusion
  177.6 9.2 %copy.95 = f32[1024,2048]{1,0:T(8,128)} copy(f32[1024,2048]{0,1:T(8,128)} %pad_maximum_fusion) | data formatting | bytes 16777216
  187.5 0.8 copy-done.3
  188.4 1.4 fusion.37
  189.8 223.7 %reduce-scatter.7.cloned.1.call-done = f32[32,2048]{1,0:T(8,128)} async-done(((f32[1024,2048]{1,0:T(8,128)}), f32[32,2048]{1,0:T(8,128)}) %reduce-scatter.7.cloned.1.call-update) | async-done | bytes 262160
  413.5 0.9 slice.55
  414.7 3.5 gather_fusion.3
  418.1 9.3 %fusion.11 = f32[32,512,128]{2,0,1:T(8,128)S(1)} fusion(bf16[512,128,128]{2,1,0:T(8,128)(2,1)} %param.19, bf16[512,32,128]{2,1,0:T(8,128)(2,1)} %gather_fusion.3), kind=kOutput, calls=%fused_computation.16 | convolution fusion | flops 536870912 | bytes 29360128 | tf_op jit(solution)/shard_map/fki,kij->fkj/dot_general | solution.py:83
  427.5 9.6 %fusion = f32[48,32,128]{2,0,1:T(8,128)S(1)} fusion(f32[32,512,128]{2,0,1:T(8,128)S(1)} %fusion.11, f32[512]{0:T(512)S(1)} %fusion.30, s32[512]{0:T(512)S(1)} %copy-done.7), kind=kOutput, calls=%fused_computation.7 | convolution fusion | flops 1208008704 | bytes 9179136 | tf_op jit(solution)/shard_map/fkj,kt->ftj/dot_general | solution.py:84
  438.0 4.3 all-to-all-start.1
  443.3 1.4 fusion.36
  444.7 15.9 %psum.23 = f32[32]{0:T(128)} all-reduce(f32[32]{0:T(128)S(1)} %get-tuple-element.54), channel_id=1, replica_groups=mesh['dom'=8,'feat'=32] {'dom'}, use_global_device_ids=true, to_apply=%region_8.9 | all-reduce | flops 32 | bytes 256 | tf_op jit(solution)/shard_map/psum | solution.py:71
  461.9 7.0 %scatter_fusion = f32[32,4096]{0,1:T(8,128)S(1)} fusion(f32[32,4096]{0,1:T(8,128)S(1)} %copy.99, s32[1024]{0:T(1024)S(1)} %get-tuple-element.59, f32[1024,32]{1,0:T(8,128)S(1)} %copy.90), kind=kCustom, calls=%fused_computation.4 | custom fusion | flops 32768 | bytes 397312 | tf_op jit(solution)/shard_map/scatter-add | solution.py:95
  469.0 9.9 %reduce-scatter.9.cloned.1.call-done = bf16[128,32]{1,0:T(8,128)(2,1)} async-done(((bf16[1024,32]{1,0:T(8,128)(2,1)}), bf16[128,32]{1,0:T(8,128)(2,1)}) %reduce-scatter.9.cloned.1.call-update) | async-done | bytes 8208
  479.8 2.0 scatter_fusion.1
  482.6 1.4 copy.92
  484.0 61.6 %all-reduce.3.cloned.1.call-done = (f32[32,1024]{1,0:T(8,128)}, f32[32,1024]{1,0:T(8,128)}) async-done(((f32[32,1024]{1,0:T(8,128)}, f32[32,1024]{1,0:T(8,128)}), (f32[32,1024]{1,0:T(8,128)}, f32[32,1024]{1,0:T(8,128)})) %all-reduce.3.cloned.1.call-update) | async-done | bytes 262160 | tf_op jit(solution)/shard_map/psum | solution.py:71
  545.6 1.6 copy.132
  547.2 1.6 copy.133
  (67 shorter events, 13.5 us)
Async XLA Ops:
  7.2 162.0 %copy-start = (bf16[32,1024]{1,0:T(8,128)(2,1)S(1)}, bf16[32,1024]{1,0:T(8,128)(2,1)}, u32[]{:S(2)}) copy-start(bf16[32,1024]{1,0:T(8,128)(2,1)} %param.21) | copy-start | bytes 196612
  7.2 83.7 %all-gather.3.cloned.1.call-start = ((), (), s32[]{:S(2)}) async-start(), calls=%async_computation.4 | async-start | bytes 2162688 | tf_op jit(solution)/shard_map/all_gather | solution.py:55
  15.5 21.8 %all-to-all-start = ((bf16[32,8,128]{2,0,1:T(8,128)(2,1)}), bf16[32,8,128]{2,0,1:T(8,128)(2,1)S(1)}, u32[]{:S(2)}, u32[]{:S(2)}) async-start(bf16[32,8,128]{2,0,1:T(8,128)(2,1)} %broadcast_select_fusion), calls=%async_computation | async-start | bytes 131072 | tf_op jit(solution)/shard_map/all_to_all | solution.py:37
  20.0 149.2 %all-gather.5.cloned.1.call-start = ((), (), s32[]{:S(2)}) async-start(), calls=%async_computation.5 | async-start | bytes 2162688 | tf_op jit(solution)/shard_map/all_gather | solution.py:56
  41.8 13.0 %copy-start.6 = (s32[512]{0:T(512)S(1)}, s32[512]{0:T(512)}, u32[]{:S(2)}) copy-start(s32[512]{0:T(512)} %param.16) | copy-start | bytes 6148
  54.8 36.1 %copy-start.4 = (bf16[32,1024]{1,0:T(8,128)(2,1)S(1)}, bf16[32,1024]{1,0:T(8,128)(2,1)}, u32[]{:S(2)}) copy-start(bf16[32,1024]{1,0:T(8,128)(2,1)} %param.20) | copy-start | bytes 196612
  54.8 114.4 %copy-start.5 = (bf16[32,1024]{1,0:T(8,128)(2,1)S(1)}, bf16[32,1024]{1,0:T(8,128)(2,1)}, u32[]{:S(2)}) copy-start(bf16[32,1024]{1,0:T(8,128)(2,1)} %param.23) | copy-start | bytes 196612
  54.8 114.4 %copy-start.8 = (f32[32]{0:T(128)S(1)}, f32[32]{0:T(128)}, u32[]{:S(2)}) copy-start(f32[32]{0:T(128)} %param.22) | copy-start | bytes 388
  64.1 349.3 %reduce-scatter.7.cloned.1.call-start = ((), (), s32[]{:S(2)}) async-start(), calls=%async_computation.6 | async-start | bytes 8650752
  186.8 1.6 copy-start.3
  418.1 9.3 %copy-start.7 = (s32[512]{0:T(512)S(1)}, s32[512]{0:T(512)}, u32[]{:S(2)}) copy-start(s32[512]{0:T(512)} %param.17) | copy-start | bytes 6148
  427.5 15.8 %copy-start.2 = (bf16[1024,1024]{1,0:T(8,128)(2,1)S(1)}, bf16[1024,1024]{1,0:T(8,128)(2,1)}, u32[]{:S(2)}) copy-start(bf16[1024,1024]{1,0:T(8,128)(2,1)} %all-gather.3.cloned.1.call-done) | copy-start | bytes 6291460
  437.1 23.7 %slice-start = ((f32[32,2048]{1,0:T(8,128)}), f32[32,1024]{1,0:T(8,128)S(1)}, s32[]{:S(2)}) async-start(f32[32,2048]{1,0:T(8,128)} %reduce-scatter.7.cloned.1.call-done), calls=%async_computation.9 | async-start | bytes 262144 | tf_op jit(solution)/shard_map/slice | solution.py:80
  438.0 23.7 %all-to-all-start.1 = ((bf16[32,8,128]{2,0,1:T(8,128)(2,1)}), bf16[32,8,128]{2,0,1:T(8,128)(2,1)S(1)}, u32[]{:S(2)}, u32[]{:S(2)}) async-start(bf16[32,8,128]{2,0,1:T(8,128)(2,1)} %bitcast.91), calls=%async_computation.1 | async-start | bytes 131072 | tf_op jit(solution)/shard_map/all_to_all | solution.py:88
  442.3 36.5 %reduce-scatter.9.cloned.1.call-start = ((), (), s32[]{:S(2)}) async-start(), calls=%async_computation.7 | async-start | bytes 294912
  443.2 102.4 %all-reduce.3.cloned.1.call-start = ((), (), s32[]{:S(2)}) async-start(), calls=%async_computation.8 | async-start | bytes 524288 | tf_op jit(solution)/shard_map/psum | solution.py:71
  461.1 87.7 %copy-start.1 = (bf16[32,1024]{1,0:T(8,128)(2,1)S(1)}, bf16[32,1024]{1,0:T(8,128)(2,1)}, u32[]{:S(2)}) copy-start(bf16[32,1024]{1,0:T(8,128)(2,1)} %param.21) | copy-start | bytes 196612
Sparse Core Ops, SparseCore 0:
  11.2 79.6 all-gather.2
  94.1 75.1 all-gather.4
  186.9 226.4 reduce-scatter.6
  446.1 32.6 reduce-scatter.8
  481.6 63.9 all-reduce.2
where the time goes:
time: 556 us; the launch traced here: 555 us
  waiting for transfers between devices  398 us (72%)
  matrix products  49.6 us (9%)
  local copies, waits for them, and re-layouts  34.4 us (6%)
  blocking collectives  29.5 us (5%)
  other arithmetic  19.8 us (4%)
  between operations  14.7 us (3%)
  starting transfers between devices  9.13 us (2%)
    unnamed x7, waiting for transfers between devices  234 us
    all_gather x1, waiting for transfers between devices, body(): lax.all_gather(aggregate, 'feat', axis=0, tiled=True)  76.2 us
    psum x1, waiting for transfers between devices, body(): lax.psum((local_self, local_neigh, local_bias), 'dom')  61.6 us
    all_gather x1, waiting for transfers between devices, body(): lax.all_gather(dst_feats, 'feat', axis=0, tiled=True)  26.6 us
    unnamed x31, local copies, waits for them, and re-layouts  19.8 us
    psum x1, blocking collectives, body(): lax.psum((local_self, local_neigh, local_bias), 'dom')  15.9 us
    all_gather x1, blocking collectives, body(): lax.all_gather(jnp.take(node_feats, hub_rows, axis=1), 'dom', axis=1, til...  13.7 us
    dot_general x1, matrix products, body(): jnp.einsum('fkj,kij->fki', picked, tile_vals, preferred_element_type=jnp....  13 us
  transfers between devices with their start and end apart: 7, of which 5 were waited for; matrix products, arithmetic and copies ran while one was open for 10% of the time, Pallas kernels for 0%

commit v1 on v0

--- a/solution.py
+++ b/solution.py
@@ -1,7 +1,22 @@
+import functools
 import jax
 import jax.numpy as jnp
 from jax import lax
 from jax.sharding import PartitionSpec as P
+from jax.lax import all_to_all, axis_size
+
+
+def _use_rails(view, a_name):
+    slots = []
+    for _ in range(axis_size(a_name)):
+        slots.append(view)
+    big = jnp.stack(slots)
+    m_next = all_to_all(big, a_name, split_axis=0, concat_axis=0)
+    before = jnp.concatenate(m_next, 0)
+    return before
+
+
+meshes_test = functools.partial(_use_rails, a_name="feat")
 
 
 def contract_first(left, right):
@@ -53,7 +68,7 @@
     dst_feats = node_feats[:, :dst_rows]
     whole_self, whole_agg = (
         lax.all_gather(dst_feats, "feat", axis=0, tiled=True),
-        lax.all_gather(aggregate, "feat", axis=0, tiled=True),
+        meshes_test(aggregate),
     )
     pre_act = (
         jnp.dot(w_self, whole_self, preferred_element_type=jnp.float32)

time: 556 us -> 515 us (0.926)
  waiting for transfers between devices: 398 us -> 347 us
  starting transfers between devices: 9.13 us -> 20.5 us
    all_gather x1 -> x0, waiting for transfers between devices: 76.2 us -> none  [body(): lax.all_gather(aggregate, 'feat', axis=0, tiled=True)]
    all_to_all x0 -> x1, waiting for transfers between devices: none -> 33.4 us  [_use_rails(): m_next = all_to_all(big, a_name, split_axis=0, concat_axis=0)]
    all_to_all x0 -> x1, starting transfers between devices: none -> 11.6 us  [_use_rails(): m_next = all_to_all(big, a_name, split_axis=0, concat_axis=0)]
    all_gather x1, waiting for transfers between devices: 26.6 us -> 18.6 us  [body(): lax.all_gather(dst_feats, 'feat', axis=0, tiled=True)]
    unnamed x31 -> x29, local copies, waits for them, and re-layouts: 19.8 us -> 18.3 us
    unnamed x7 -> x6, waiting for transfers between devices: 234 us -> 233 us
  transfers between devices with their start and end apart: 7 -> 7, of which waited for: 5 -> 5; matrix products, arithmetic and copies ran while one was open for 10% -> 11% of each run, Pallas kernels for 0% -> 0%
where the time goes in v1:
time: 515 us; the launch traced here: 514 us
  waiting for transfers between devices  347 us (67%)
  matrix products  48.3 us (9%)
  local copies, waits for them, and re-layouts  34.5 us (7%)
  blocking collectives  29.5 us (6%)
  starting transfers between devices  20.5 us (4%)
  other arithmetic  19.8 us (4%)
  between operations  14.7 us (3%)
    unnamed x6, waiting for transfers between devices  233 us
    psum x1, waiting for transfers between devices, body(): lax.psum((local_self, local_neigh, local_bias), 'dom')  61.7 us
    all_to_all x1, waiting for transfers between devices, _use_rails(): m_next = all_to_all(big, a_name, split_axis=0, concat_axis=0)  33.4 us
    all_gather x1, waiting for transfers between devices, body(): lax.all_gather(dst_feats, 'feat', axis=0, tiled=True)  18.6 us
    unnamed x29, local copies, waits for them, and re-layouts  18.3 us
    psum x1, blocking collectives, body(): lax.psum((local_self, local_neigh, local_bias), 'dom')  15.9 us
    all_gather x1, blocking collectives, body(): lax.all_gather(jnp.take(node_feats, hub_rows, axis=1), 'dom', axis=1, til...  13.7 us
    dot_general x1, matrix products, body(): jnp.einsum('fkj,kij->fki', picked, tile_vals, preferred_element_type=jnp....  13 us
  transfers between devices with their start and end apart: 7, of which 5 were waited for; matrix products, arithmetic and copies ran while one was open for 11% of the time, Pallas kernels for 0%

profile of v1, /device:TPU:2, one launch (start us, length us, event | category | flops | bytes accessed | tf_op | source)
XLA Modules:
  0.0 514.0 jit_solution(10461168480133183761)
XLA Ops:
  7.2 1.5 slice.40
  10.1 1.4 copy.77
  11.5 3.2 gather_fusion
  15.5 4.5 all-to-all-start
  23.5 13.7 %all_gather.7 = bf16[32,1024]{0,1:T(8,128)(2,1)S(1)} all-gather(bf16[32,128]{0,1:T(8,128)(2,1)S(1)} %select_bitcast_fusion), channel_id=1, replica_groups=mesh['dom'=8,'feat'=32] {'dom'}, dimensions={1}, use_global_device_ids=true | all-gather | bytes 73728 | tf_op jit(solution)/shard_map/all_gather | solution.py:53
  37.3 1.0 copy_bitcast_fusion.1
  38.4 3.5 gather_fusion.2
  41.8 13.0 %fusion.8 = f32[32,512,128]{2,0,1:T(8,128)S(1)} fusion(bf16[512,128,128]{2,1,0:T(8,128)(2,1)} %param.19, bf16[512,32,128]{2,1,0:T(8,128)(2,1)} %gather_fusion.2), kind=kOutput, calls=%fused_computation.15 | convolution fusion | flops 536870912 | bytes 29360128 | tf_op jit(solution)/shard_map/fkj,kij->fki/dot_general | solution.py:65
  54.8 8.6 %fusion.16 = bf16[8,32,128]{2,0,1:T(8,128)(2,1)S(1)} fusion(f32[32,512,128]{2,0,1:T(8,128)S(1)} %fusion.8, f32[512]{0:T(512)S(1)} %fusion.30, s32[512]{0:T(512)S(1)} %copy-done.5), kind=kOutput, calls=%fused_computation.22 | convolution fusion | flops 201367552 | bytes 8458240 | tf_op jit(solution)/shard_map/fki,ku->fui/dot_general | solution.py:66
  63.5 1.6 stack.2
  65.1 11.6 %all-to-all-start.1 = ((bf16[32,32,1024]{2,1,0:T(8,128)(2,1)}), bf16[32,32,1024]{2,1,0:T(8,128)(2,1)S(1)}, u32[]{:S(2)}, u32[]{:S(2)}) async-start(bf16[32,32,1024]{2,1,0:T(8,128)(2,1)} %stack.2), calls=%async_computation.1 | async-start | bytes 4194304 | tf_op jit(solution)/shard_map/all_to_all | solution.py:14
  76.7 18.6 %all-gather.2.cloned.1.call-done = bf16[1024,1024]{1,0:T(8,128)(2,1)} async-done(((bf16[32,1024]{1,0:T(8,128)(2,1)}), bf16[1024,1024]{1,0:T(8,128)(2,1)}) %all-gather.2.cloned.1.call-update) | async-done | bytes 2097168 | tf_op jit(solution)/shard_map/all_gather | solution.py:70
  95.3 2.1 fusion.35
  97.4 33.4 %all-to-all-done.1 = bf16[32,32,1024]{2,1,0:T(8,128)(2,1)S(1)} async-done(((bf16[32,32,1024]{2,1,0:T(8,128)(2,1)}), bf16[32,32,1024]{2,1,0:T(8,128)(2,1)S(1)}, u32[]{:S(2)}, u32[]{:S(2)}) %all-to-all-start.1) | async-done | bytes 2097184 | tf_op jit(solution)/shard_map/all_to_all | solution.py:14
  130.8 1.2 convert_reduce_fusion
  133.5 4.1 pad_maximum_fusion
  137.6 9.2 %copy.95 = f32[1024,2048]{1,0:T(8,128)} copy(f32[1024,2048]{0,1:T(8,128)} %pad_maximum_fusion) | data formatting | bytes 16777216
  147.5 1.4 fusion.37
  148.9 222.8 %reduce-scatter.7.cloned.1.call-done = f32[32,2048]{1,0:T(8,128)} async-done(((f32[1024,2048]{1,0:T(8,128)}), f32[32,2048]{1,0:T(8,128)}) %reduce-scatter.7.cloned.1.call-update) | async-done | bytes 262160
  372.8 3.5 gather_fusion.3
  376.3 9.5 %fusion.11 = f32[32,512,128]{2,0,1:T(8,128)S(1)} fusion(bf16[512,128,128]{2,1,0:T(8,128)(2,1)} %param.19, bf16[512,32,128]{2,1,0:T(8,128)(2,1)} %gather_fusion.3), kind=kOutput, calls=%fused_computation.16 | convolution fusion | flops 536870912 | bytes 29360128 | tf_op jit(solution)/shard_map/fki,kij->fkj/dot_general | solution.py:98
  385.9 9.6 %fusion = f32[48,32,128]{2,0,1:T(8,128)S(1)} fusion(f32[32,512,128]{2,0,1:T(8,128)S(1)} %fusion.11, f32[512]{0:T(512)S(1)} %fusion.30, s32[512]{0:T(512)S(1)} %copy-done.6), kind=kOutput, calls=%fused_computation.7 | convolution fusion | flops 1208008704 | bytes 9179136 | tf_op jit(solution)/shard_map/fkj,kt->ftj/dot_general | solution.py:99
  396.4 4.3 all-to-all-start.2
  401.6 1.4 fusion.36
  403.1 15.9 %psum.23 = f32[32]{0:T(128)} all-reduce(f32[32]{0:T(128)S(1)} %get-tuple-element.54), channel_id=1, replica_groups=mesh['dom'=8,'feat'=32] {'dom'}, use_global_device_ids=true, to_apply=%region_8.9 | all-reduce | flops 32 | bytes 256 | tf_op jit(solution)/shard_map/psum | solution.py:86
  420.3 7.1 %scatter_fusion = f32[32,4096]{0,1:T(8,128)S(1)} fusion(f32[32,4096]{0,1:T(8,128)S(1)} %copy.99, s32[1024]{0:T(1024)S(1)} %get-tuple-element.59, f32[1024,32]{1,0:T(8,128)S(1)} %copy.90), kind=kCustom, calls=%fused_computation.4 | custom fusion | flops 32768 | bytes 397312 | tf_op jit(solution)/shard_map/scatter-add | solution.py:110
  427.3 10.1 %reduce-scatter.9.cloned.1.call-done = bf16[128,32]{1,0:T(8,128)(2,1)} async-done(((bf16[1024,32]{1,0:T(8,128)(2,1)}), bf16[128,32]{1,0:T(8,128)(2,1)}) %reduce-scatter.9.cloned.1.call-update) | async-done | bytes 8208
  438.4 2.0 scatter_fusion.1
  441.2 1.4 copy.92
  442.6 61.7 %all-reduce.3.cloned.1.call-done = (f32[32,1024]{1,0:T(8,128)}, f32[32,1024]{1,0:T(8,128)}) async-done(((f32[32,1024]{1,0:T(8,128)}, f32[32,1024]{1,0:T(8,128)}), (f32[32,1024]{1,0:T(8,128)}, f32[32,1024]{1,0:T(8,128)})) %all-reduce.3.cloned.1.call-update) | async-done | bytes 262160 | tf_op jit(solution)/shard_map/psum | solution.py:86
  504.3 1.6 copy.132
  505.9 1.6 copy.133
  (65 shorter events, 13.5 us)
Async XLA Ops:
  7.2 123.6 %copy-start = (bf16[32,1024]{1,0:T(8,128)(2,1)S(1)}, bf16[32,1024]{1,0:T(8,128)(2,1)}, u32[]{:S(2)}) copy-start(bf16[32,1024]{1,0:T(8,128)(2,1)} %param.21) | copy-start | bytes 196612
  7.2 88.2 %all-gather.2.cloned.1.call-start = ((), (), s32[]{:S(2)}) async-start(), calls=%async_computation.5 | async-start | bytes 2162688 | tf_op jit(solution)/shard_map/all_gather | solution.py:70
  15.5 21.8 %all-to-all-start = ((bf16[32,8,128]{2,0,1:T(8,128)(2,1)}), bf16[32,8,128]{2,0,1:T(8,128)(2,1)S(1)}, u32[]{:S(2)}, u32[]{:S(2)}) async-start(bf16[32,8,128]{2,0,1:T(8,128)(2,1)} %broadcast_select_fusion), calls=%async_computation | async-start | bytes 131072 | tf_op jit(solution)/shard_map/all_to_all | solution.py:52
  41.8 13.0 %copy-start.5 = (s32[512]{0:T(512)S(1)}, s32[512]{0:T(512)}, u32[]{:S(2)}) copy-start(s32[512]{0:T(512)} %param.16) | copy-start | bytes 6148
  63.4 31.9 %copy-start.3 = (bf16[32,1024]{1,0:T(8,128)(2,1)S(1)}, bf16[32,1024]{1,0:T(8,128)(2,1)}, u32[]{:S(2)}) copy-start(bf16[32,1024]{1,0:T(8,128)(2,1)} %param.20) | copy-start | bytes 196612
  63.4 67.3 %copy-start.4 = (bf16[32,1024]{1,0:T(8,128)(2,1)S(1)}, bf16[32,1024]{1,0:T(8,128)(2,1)}, u32[]{:S(2)}) copy-start(bf16[32,1024]{1,0:T(8,128)(2,1)} %param.23) | copy-start | bytes 196612
  63.4 67.3 %copy-start.7 = (f32[32]{0:T(128)S(1)}, f32[32]{0:T(128)}, u32[]{:S(2)}) copy-start(f32[32]{0:T(128)} %param.22) | copy-start | bytes 388
  65.1 65.7 %all-to-all-start.1 = ((bf16[32,32,1024]{2,1,0:T(8,128)(2,1)}), bf16[32,32,1024]{2,1,0:T(8,128)(2,1)S(1)}, u32[]{:S(2)}, u32[]{:S(2)}) async-start(bf16[32,32,1024]{2,1,0:T(8,128)(2,1)} %stack.2), calls=%async_computation.1 | async-start | bytes 4194304 | tf_op jit(solution)/shard_map/all_to_all | solution.py:14
  76.7 294.9 %reduce-scatter.7.cloned.1.call-start = ((), (), s32[]{:S(2)}) async-start(), calls=%async_computation.6 | async-start | bytes 8650752
  376.3 9.5 %copy-start.6 = (s32[512]{0:T(512)S(1)}, s32[512]{0:T(512)}, u32[]{:S(2)}) copy-start(s32[512]{0:T(512)} %param.17) | copy-start | bytes 6148
  385.8 15.8 %copy-start.2 = (bf16[1024,1024]{1,0:T(8,128)(2,1)S(1)}, bf16[1024,1024]{1,0:T(8,128)(2,1)}, u32[]{:S(2)}) copy-start(bf16[1024,1024]{1,0:T(8,128)(2,1)} %all-gather.2.cloned.1.call-done) | copy-start | bytes 6291460
  395.5 23.7 %slice-start = ((f32[32,2048]{1,0:T(8,128)}), f32[32,1024]{1,0:T(8,128)S(1)}, s32[]{:S(2)}) async-start(f32[32,2048]{1,0:T(8,128)} %reduce-scatter.7.cloned.1.call-done), calls=%async_computation.9 | async-start | bytes 262144 | tf_op jit(solution)/shard_map/slice | solution.py:95
  396.4 23.6 %all-to-all-start.2 = ((bf16[32,8,128]{2,0,1:T(8,128)(2,1)}), bf16[32,8,128]{2,0,1:T(8,128)(2,1)S(1)}, u32[]{:S(2)}, u32[]{:S(2)}) async-start(bf16[32,8,128]{2,0,1:T(8,128)(2,1)} %bitcast.92), calls=%async_computation.2 | async-start | bytes 131072 | tf_op jit(solution)/shard_map/all_to_all | solution.py:103
  400.7 36.8 %reduce-scatter.9.cloned.1.call-start = ((), (), s32[]{:S(2)}) async-start(), calls=%async_computation.7 | async-start | bytes 294912
  401.6 102.7 %all-reduce.3.cloned.1.call-start = ((), (), s32[]{:S(2)}) async-start(), calls=%async_computation.8 | async-start | bytes 524288 | tf_op jit(solution)/shard_map/psum | solution.py:86
  419.4 88.0 %copy-start.1 = (bf16[32,1024]{1,0:T(8,128)(2,1)S(1)}, bf16[32,1024]{1,0:T(8,128)(2,1)}, u32[]{:S(2)}) copy-start(bf16[32,1024]{1,0:T(8,128)(2,1)} %param.21) | copy-start | bytes 196612
Sparse Core Ops, SparseCore 0:
  11.2 84.1 all-gather.1
  146.9 224.6 reduce-scatter.6
  404.7 32.6 reduce-scatter.8
  440.3 63.9 all-reduce.2
